TPU v7x, 32 devices: a whole 2x2x4 slice. The times are simulated.
32 devices in a mesh: macro: 4 (over y, x), micro: 8 (over z, core).
Axes of the slice: x: 2, y: 2, z: 4, core: 2. Of those that a mesh axis runs over, the one named last changes fastest.
Arguments:
- displacement: float32 [3, 8, 16, 256], P(None, 'macro', 'micro'), may hold values from -6 to 6
- load: float32 [3, 8, 16, 256], P(None, 'macro', 'micro'), may hold values from -6 to 6
- routes: int32 [4, 8, 1024, 1], P('macro', 'micro'), may hold values from 0 to 7; in each aligned block of 1024 rows (0 to 1023, 1024 to 2047, ..., all dimensions but the last counted through in order) at most 256 rows name the same one
- counts: int32 [4, 8, 1024], P('macro', 'micro'), may hold values from 1 to 4
- stiffness: bfloat16 [8, 512, 512], P('micro'), may hold values from -0.5 to 2.5, as said below
- precond: bfloat16 [8, 512, 512], P('micro'), may hold values from -0.5 to 2.5, as said below
- forcing: bfloat16 [8, 6, 512], P('micro'), may hold values from -2.5 to 2.5
- coupling: bfloat16 [8, 512, 6], P('micro'), may hold values from -0.25 to 0.25
- lame_first: float32 [8], P('micro'), may hold values from 0.5 to 2
- lame_shear: float32 [8], P('micro'), may hold values from 0.5 to 2
Outputs:
- increment: float32 [3, 8, 16, 256], P(None, 'macro', 'micro')
- residual: float32 [3, 8, 16, 256], P(None, 'macro', 'micro')
Inputs may be any that keep to these rules, and one draw needn't show every extreme that they name: `routes`: among the points of one block (one device's points), no owner is named by more than 256 points, a bound that some block reaches. `stiffness`: Symmetric. `precond`: Symmetric.
All inputs are finite; a program needn't handle non-finite values.
Results may differ from a plain program's by a relative error of at most 0.002.
Values sent between devices are 32-bit elements; how exact they have to be, the bound alone decides.
A program may use at most 64 MiB of HBM per device.

v0:
```python
import jax
import jax.numpy as jnp
from jax import lax
from jax.sharding import PartitionSpec as P

ITMAX = 4
ITERS = 5
BETA = 0.1
OMEGA = 0.8
MASS = 0.1
VOIGT = ((0, 5, 4), (5, 1, 3), (4, 3, 2))
ALL_PAIRS = tuple(
    ((first_axis, second_axis) for first_axis in range(6) for second_axis in range(6))
)


def with_halo(block, sides, width):
    for axis, dim in sides:
        count = lax.axis_size(axis)
        forward = [(i, i + 1) for i in range(count - 1)]
        backward = [(target, source) for source, target in forward]
        low = lax.ppermute(
            lax.slice_in_dim(block, block.shape[dim] - width, None, axis=dim), axis, forward
        )
        high = lax.ppermute(lax.slice_in_dim(block, 0, width, axis=dim), axis, backward)
        block = jnp.concatenate([low, block, high], axis=dim)
    return block


def passed_along(value, axis, steps):
    count = lax.axis_size(axis)
    initial, last = (max(0, -steps), min(count, count - steps))
    return lax.ppermute(value, axis, [(source, source + steps) for source in range(initial, last)])


def element_strain(nodes):
    count_x = nodes.shape[1] - 1
    count_y = nodes.shape[2] - 1
    count_z = nodes.shape[3]
    padded = jnp.pad(nodes, ((0, 0), (0, 0), (0, 0), (0, 1)))
    zeros = jnp.zeros((3, count_x, count_y, count_z), jnp.float32)
    grad_x, grad_y, grad_z = (zeros, zeros, zeros)
    for corner_x in (0, 1):
        for corner_y in (0, 1):
            for corner_z in (0, 1):
                piece = padded[
                    :,
                    corner_x : corner_x + count_x,
                    corner_y : corner_y + count_y,
                    corner_z : corner_z + count_z,
                ]
                grad_x = grad_x + 0.25 * (2 * corner_x - 1) * piece
                grad_y = grad_y + 0.25 * (2 * corner_y - 1) * piece
                grad_z = grad_z + 0.25 * (2 * corner_z - 1) * piece
    return jnp.stack(
        [
            grad_x[0],
            grad_y[1],
            grad_z[2],
            grad_z[1] + grad_y[2],
            grad_z[0] + grad_x[2],
            grad_y[0] + grad_x[1],
        ]
    )


def node_force(stress):
    count_x, count_y, count_z = (stress.shape[1], stress.shape[2], stress.shape[3])
    forces = jnp.zeros((3, count_x + 1, count_y + 1, count_z + 1), jnp.float32)
    for corner_x in (0, 1):
        for corner_y in (0, 1):
            for corner_z in (0, 1):
                signs = (2 * corner_x - 1, 2 * corner_y - 1, 2 * corner_z - 1)
                parts = []
                for component in range(3):
                    table = VOIGT[component]
                    parts.append(
                        0.25
                        * (
                            signs[0] * stress[table[0]]
                            + signs[1] * stress[table[1]]
                            + signs[2] * stress[table[2]]
                        )
                    )
                contrib = jnp.stack(parts)
                forces = forces + jnp.pad(
                    contrib,
                    (
                        (0, 0),
                        (corner_x, 1 - corner_x),
                        (corner_y, 1 - corner_y),
                        (corner_z, 1 - corner_z),
                    ),
                )
    return forces


def micro_solve(
    strain, sweeps, stiffness, precond, forcing, coupling, lame_first, lame_shear, pairs
):
    strain_half = strain.astype(jnp.bfloat16)
    modal_load = lax.dot_general(
        strain_half, forcing, (((0,), (0,)), ((), ())), preferred_element_type=jnp.float32
    )
    modes = jnp.zeros_like(modal_load)
    for sweep in range(ITMAX):
        misfit = (
            jnp.dot(modes.astype(jnp.bfloat16), stiffness, preferred_element_type=jnp.float32)
            + BETA * jnp.tanh(modes)
            - modal_load
        )
        update = modes - OMEGA * jnp.dot(
            misfit.astype(jnp.bfloat16), precond, preferred_element_type=jnp.float32
        )
        modes = jnp.where((sweeps[0] > sweep)[:, None], update, modes)
    trace = strain[0] + strain[1] + strain[2]
    elastic = jnp.stack(
        [
            lame_first * trace + 2.0 * lame_shear * strain[0],
            lame_first * trace + 2.0 * lame_shear * strain[1],
            lame_first * trace + 2.0 * lame_shear * strain[2],
            lame_shear * strain[3],
            lame_shear * strain[4],
            lame_shear * strain[5],
        ]
    )
    stress = elastic + lax.dot_general(
        coupling,
        modes.astype(jnp.bfloat16),
        (((0,), (1,)), ((), ())),
        preferred_element_type=jnp.float32,
    )
    slope = 1.0 - jnp.tanh(modes) ** 2
    wide = coupling.astype(jnp.float32)
    products = jnp.stack([wide[:, pair[0]] * wide[:, pair[1]] for pair in pairs], axis=1)
    extra = lax.dot_general(
        products,
        slope,
        (((0,), (1,)), ((), ())),
        precision=lax.Precision.HIGHEST,
        preferred_element_type=jnp.float32,
    )
    base = jnp.stack(
        [
            lame_first * float(pair[0] < 3 and pair[1] < 3)
            + lame_shear
            * (
                2.0 * float(pair[0] == pair[1] and pair[0] < 3)
                + float(pair[0] == pair[1] and pair[0] >= 3)
            )
            for pair in pairs
        ]
    )
    return jnp.concatenate([stress, extra + base[:, None]], axis=0)


def extend(field):
    return with_halo(field, (("macro", 1), ("micro", 2)), 1)


def operate(field, tangent_ext):
    strain = element_strain(extend(field))
    stress = jnp.sum(tangent_ext * strain[None], axis=1)
    return MASS * field + node_force(stress)[:, 1:-1, 1:-1, :-1]


def two_products(residual, image):
    return lax.psum((jnp.sum(residual * residual), jnp.sum(residual * image)), ("macro", "micro"))


def shards(
    displacement,
    load,
    routes,
    counts,
    stiffness,
    precond,
    forcing,
    coupling,
    lame_first,
    lame_shear,
):
    count_x, count_y, count_z = (
        displacement.shape[1],
        displacement.shape[2],
        displacement.shape[3],
    )
    points = count_x * count_y * count_z
    owners = lax.axis_size("micro")
    capacity = max(2, 2 * points // owners)
    strain_ext = element_strain(extend(displacement))
    strain_points = strain_ext[:, 1:, 1:].reshape(6, points)
    owner_of = routes.reshape(points)
    sweeps_of = counts.reshape(points)
    onehot = (owner_of[:, None] == jnp.arange(owners, dtype=jnp.int32)[None, :]).astype(jnp.int32)
    ranks = jnp.sum((jnp.cumsum(onehot, axis=0) - 1) * onehot, axis=1)
    target = owner_of * capacity + ranks
    send_strain = jnp.zeros((6, owners * capacity), jnp.float32).at[:, target].set(strain_points)
    send_sweeps = jnp.zeros((1, owners * capacity), jnp.int32).at[0, target].set(sweeps_of)
    got_strain, got_sweeps = (
        lax.all_to_all(send_strain, "micro", split_axis=1, concat_axis=1, tiled=True),
        lax.all_to_all(send_sweeps, "micro", split_axis=1, concat_axis=1, tiled=True),
    )
    rows = micro_solve(
        got_strain,
        got_sweeps,
        stiffness[0],
        precond[0],
        forcing[0],
        coupling[0],
        lame_first[0],
        lame_shear[0],
        ALL_PAIRS,
    )
    back = lax.all_to_all(rows, "micro", split_axis=1, concat_axis=1, tiled=True)
    values = jnp.take(back, target, axis=1)
    values = values.reshape(42, count_x, count_y, count_z)
    left_x = passed_along(values[:, -1:], "macro", 1)
    values = jnp.concatenate([left_x, values], axis=1)
    left_y = passed_along(values[:, :, -1:], "micro", 1)
    values = jnp.concatenate([left_y, values], axis=2)
    stress_ext = values[:6]
    tangent_ext = values[6:].reshape(6, 6, count_x + 1, count_y + 1, count_z)
    rhs = load - node_force(stress_ext)[:, 1:-1, 1:-1, :-1]

    def apply(field):
        return operate(field, tangent_ext)

    increment = jnp.zeros_like(rhs)
    residual = rhs
    image = apply(residual)
    norm_now, product = two_products(residual, image)
    alpha = norm_now / product
    direction, along = (residual, image)
    for step in range(ITERS):
        increment = increment + alpha * direction
        residual = residual - alpha * along
        if step + 1 < ITERS:
            image = apply(residual)
            norm_next, product = two_products(residual, image)
            ratio = norm_next / norm_now
            alpha = norm_next / (product - ratio * norm_next / alpha)
            direction = residual + ratio * direction
            along = image + ratio * along
            norm_now = norm_next
    return (increment, residual)


def solution(mesh):
    in_specs = (
        P(None, "macro", "micro", None),
        P(None, "macro", "micro", None),
        P("macro", "micro", None, None),
        P("macro", "micro", None),
        P("micro", None, None),
        P("micro", None, None),
        P("micro", None, None),
        P("micro", None, None),
        P("micro"),
        P("micro"),
    )
    out_specs = (P(None, "macro", "micro", None), P(None, "macro", "micro", None))
    return jax.shard_map(shards, mesh=mesh, in_specs=in_specs, out_specs=out_specs, check_vma=False)
```

profile of v0, /device:TPU:0, one launch (start us, length us, event | category | flops | bytes accessed | tf_op | source)
XLA Modules:
  0.0 446.3 jit_solution(9777166148011291204)
XLA Ops:
  1.4 4.9 %collective-permute-start = (f32[3,1,2,256]{3,2,1,0:T(2,128)S(1)}, f32[3,1,2,256]{3,2,1,0:T(2,128)S(1)}, u32[]{:S(2)}, u32[]{:S(2)}) collective-permute-start(f32[3,1,2,256]{3,2,1,0:T(2,128)S(1)} %get-tuple-element.267), channel_id=1, source_target_pairs={{0,8},{8,16},{16,24},{1,9},{9,17},{17,25},{2,10},{10,18},{18,26},{... | collective-permute-start | bytes 18440 | tf_op jit(solution)/shard_map/ppermute | solution.py:22
  14.0 5.0 %scatter_custom_fusion.1 = s32[2048]{0:T(1024)} fusion(s32[1024]{0:T(1024)S(1)} %broadcast_select_fusion.1, s32[1024]{0:T(1024)} %bitcast.117, s32[]{:T(128)} %constant.19.clone.1), kind=kCustom, calls=%fused_computation.834 | custom fusion | bytes 8704
  19.0 4.9 %all-to-all-start.1 = ((s32[1,8,256]{2,0,1:T(1,128)}), s32[1,8,256]{2,0,1:T(1,128)S(1)}, u32[]{:S(2)}, u32[]{:S(2)}) async-start(s32[1,8,256]{2,0,1:T(1,128)} %bitcast.18), calls=%async_computation.1 | async-start | bytes 16384 | tf_op jit(solution)/shard_map/all_to_all | solution.py:202
  32.9 3.3 scatter_custom_fusion
  37.2 5.7 %all-to-all-start = ((f32[6,8,256]{2,0,1:T(8,128)}), f32[6,8,256]{2,0,1:T(8,128)S(1)}, u32[]{:S(2)}, u32[]{:S(2)}) async-start(f32[6,8,256]{2,0,1:T(8,128)} %copy.26), calls=%async_computation | async-start | bytes 131072 | tf_op jit(solution)/shard_map/all_to_all | solution.py:201
  43.1 5.8 %all-to-all-done = f32[6,8,256]{2,0,1:T(8,128)S(1)} async-done(((f32[6,8,256]{2,0,1:T(8,128)}), f32[6,8,256]{2,0,1:T(8,128)S(1)}, u32[]{:S(2)}, u32[]{:S(2)}) %all-to-all-start) | async-done | bytes 49184 | tf_op jit(solution)/shard_map/all_to_all | solution.py:201
  51.6 6.6 %subtract_select_fusion.3 = f32[2048,512]{1,0:T(8,128)} fusion(pred[2048]{0:T(1024)(128)(4,1)S(1)} %gt.63, f32[2048,512]{1,0:T(8,128)} %fusion.206, bf16[1,512,512]{2,1,0:T(8,128)(2,1)S(1)} %copy-done, bf16[1,512,512]{2,1,0:T(8,128)(2,1)S(1)} %copy-done.6), kind=kOutput, calls=%fused_computation.13 | convolution fusion | flops 2152726528 | bytes 9439232 | tf_op jit(solution)/shard_map/dot_general | solution.py:112
  58.1 9.7 %subtract_select_fusion.2 = f32[2048,512]{1,0:T(8,128)} fusion(f32[2048,512]{1,0:T(8,128)} %subtract_select_fusion.3, pred[2048]{0:T(1024)(128)(4,1)S(1)} %gt.60, f32[2048,512]{1,0:T(8,128)} %fusion.206, bf16[1,512,512]{2,1,0:T(8,128)(2,1)S(1)} %copy-done, bf16[1,512,512]{2,1,0:T(8,128)(2,1)S(1)} %copy-done.6), kind=kOutput, calls=%fused_computation.5 | convolution fusion | flops 2155872256 | bytes 13633536 | tf_op jit(solution)/shard_map/dot_general | solution.py:112
  67.8 10.1 %subtract_select_fusion.1 = f32[2048,512]{1,0:T(8,128)} fusion(f32[2048,512]{1,0:T(8,128)} %subtract_select_fusion.2, pred[2048]{0:T(1024)(128)(4,1)S(1)} %gt.57, f32[2048,512]{1,0:T(8,128)} %fusion.206, bf16[1,512,512]{2,1,0:T(8,128)(2,1)S(1)} %copy-done, bf16[1,512,512]{2,1,0:T(8,128)(2,1)S(1)} %copy-done.6), kind=kOutput, calls=%fused_computation.4 | convolution fusion | flops 2155872256 | bytes 13633536 | tf_op jit(solution)/shard_map/dot_general | solution.py:112
  77.9 9.7 %subtract_select_fusion = f32[2048,512]{1,0:T(8,128)} fusion(f32[2048,512]{1,0:T(8,128)} %subtract_select_fusion.1, pred[2048]{0:T(1024)(128)(4,1)S(1)} %gt.54, f32[2048,512]{1,0:T(8,128)} %fusion.206, bf16[1,512,512]{2,1,0:T(8,128)(2,1)S(1)} %copy-done, bf16[1,512,512]{2,1,0:T(8,128)(2,1)S(1)} %copy-done.6), kind=kOutput, calls=%fused_computation.3 | convolution fusion | flops 2155872256 | bytes 13633536 | tf_op jit(solution)/shard_map/dot_general | solution.py:112
  87.8 3.0 fusion.7
  91.3 4.2 fusion.4
  96.6 3.6 all-to-all-start.2
  100.3 12.3 %all-to-all-done.2 = f32[42,8,256]{2,0,1:T(8,128)S(1)} async-done(((f32[42,8,256]{2,0,1:T(8,128)}), f32[42,8,256]{2,0,1:T(8,128)S(1)}, u32[]{:S(2)}, u32[]{:S(2)}) %all-to-all-start.2) | async-done | bytes 344096 | tf_op jit(solution)/shard_map/all_to_all | solution.py:215
  113.0 2.8 gather_fusion
  116.1 4.5 %collective-permute-start.4 = (f32[42,1,2,256]{3,2,1,0:T(2,128)S(1)}, f32[42,1,2,256]{3,2,1,0:T(2,128)S(1)}, u32[]{:S(2)}, u32[]{:S(2)}) collective-permute-start(f32[42,1,2,256]{3,2,1,0:T(2,128)S(1)} %slice.1305), channel_id=1, source_target_pairs={{0,8},{8,16},{16,24},{1,9},{9,17},{17,25},{2,10},{10,18},{18,26},{... | collective-permute-start | bytes 258056 | tf_op jit(solution)/shard_map/ppermute | solution.py:33
  126.1 4.3 collective-permute-start.6
  131.7 5.5 %collective-permute-done.7 = f32[3,1,2,256]{3,2,1,0:T(2,128)S(1)} collective-permute-done((f32[3,1,2,256]{3,2,1,0:T(2,128)S(1)}, f32[3,1,2,256]{3,2,1,0:T(2,128)S(1)}, u32[]{:S(2)}, u32[]{:S(2)}) %collective-permute-start.7) | collective-permute-done | bytes 6176 | tf_op jit(solution)/shard_map/ppermute | solution.py:25
  140.8 4.6 %collective-permute-done.9 = f32[3,4,1,256]{3,2,1,0:T(1,128)S(1)} collective-permute-done((f32[3,4,1,256]{3,2,1,0:T(1,128)S(1)}, f32[3,4,1,256]{3,2,1,0:T(1,128)S(1)}, u32[]{:S(2)}, u32[]{:S(2)}) %collective-permute-start.9) | collective-permute-done | bytes 12320 | tf_op jit(solution)/shard_map/ppermute | solution.py:25
  147.5 42.8 %all-reduce.59 = (f32[]{:T(128)}, f32[]{:T(128)}) all-reduce(f32[]{:T(128)} %get-tuple-element.11, f32[]{:T(128)} %get-tuple-element.10), channel_id=1, replica_groups=mesh['macro'=4,'micro'=8] {'macro','micro'}, use_global_device_ids=true, to_apply=%region_6.7 | all-reduce | flops 2 | bytes 16 | tf_op jit(solution)/shard_map/psum | solution.py:168
  191.6 4.2 collective-permute-start.10
  197.1 4.2 collective-permute-done.11
  208.7 42.4 %all-reduce.58 = (f32[]{:T(128)}, f32[]{:T(128)}) all-reduce(f32[]{:T(128)} %get-tuple-element.9, f32[]{:T(128)} %get-tuple-element.8), channel_id=1, replica_groups=mesh['macro'=4,'micro'=8] {'macro','micro'}, use_global_device_ids=true, to_apply=%region_11.12 | all-reduce | flops 2 | bytes 16 | tf_op jit(solution)/shard_map/psum | solution.py:168
  255.5 4.2 collective-permute-start.14
  261.0 4.2 collective-permute-done.15
  272.5 42.5 %all-reduce.57 = (f32[]{:T(128)}, f32[]{:T(128)}) all-reduce(f32[]{:T(128)} %get-tuple-element.7, f32[]{:T(128)} %get-tuple-element.6), channel_id=1, replica_groups=mesh['macro'=4,'micro'=8] {'macro','micro'}, use_global_device_ids=true, to_apply=%region_16.17 | all-reduce | flops 2 | bytes 16 | tf_op jit(solution)/shard_map/psum | solution.py:168
  318.8 4.2 collective-permute-start.18
  324.3 4.2 collective-permute-done.19
  335.9 42.4 %all-reduce.56 = (f32[]{:T(128)}, f32[]{:T(128)}) all-reduce(f32[]{:T(128)} %get-tuple-element.5, f32[]{:T(128)} %get-tuple-element.4), channel_id=1, replica_groups=mesh['macro'=4,'micro'=8] {'macro','micro'}, use_global_device_ids=true, to_apply=%region_21.22 | all-reduce | flops 2 | bytes 16 | tf_op jit(solution)/shard_map/psum | solution.py:168
  382.2 4.2 collective-permute-start.22
  387.8 4.2 collective-permute-done.23
  399.3 42.4 %all-reduce.55 = (f32[]{:T(128)}, f32[]{:T(128)}) all-reduce(f32[]{:T(128)} %get-tuple-element.3, f32[]{:T(128)} %get-tuple-element.2), channel_id=1, replica_groups=mesh['macro'=4,'micro'=8] {'macro','micro'}, use_global_device_ids=true, to_apply=%region_26.27 | all-reduce | flops 2 | bytes 16 | tf_op jit(solution)/shard_map/psum | solution.py:168
  (288 shorter events, 69.1 us)
Async XLA Ops:
  0.6 50.9 %copy-start = (bf16[1,512,512]{2,1,0:T(8,128)(2,1)S(1)}, bf16[1,512,512]{2,1,0:T(8,128)(2,1)}, u32[]{:S(2)}) copy-start(bf16[1,512,512]{2,1,0:T(8,128)(2,1)} %param.15) | copy-start | bytes 1572868
  0.6 48.2 %copy-start.5 = (bf16[1,6,512]{2,1,0:T(8,128)(2,1)S(1)}, bf16[1,6,512]{2,1,0:T(8,128)(2,1)}, u32[]{:S(2)}) copy-start(bf16[1,6,512]{2,1,0:T(8,128)(2,1)} %param.16) | copy-start | bytes 18436
  1.4 23.2 %collective-permute-start = (f32[3,1,2,256]{3,2,1,0:T(2,128)S(1)}, f32[3,1,2,256]{3,2,1,0:T(2,128)S(1)}, u32[]{:S(2)}, u32[]{:S(2)}) collective-permute-start(f32[3,1,2,256]{3,2,1,0:T(2,128)S(1)} %get-tuple-element.267), channel_id=1, source_target_pairs={{0,8},{8,16},{16,24},{1,9},{9,17},{17,25},{2,10},{10,18},{18,26},{... | collective-permute-start | bytes 18440 | tf_op jit(solution)/shard_map/ppermute | solution.py:22
  6.3 19.1 %collective-permute-start.1 = (f32[3,1,2,256]{3,2,1,0:T(2,128)S(1)}, f32[3,1,2,256]{3,2,1,0:T(2,128)S(1)}, u32[]{:S(2)}, u32[]{:S(2)}) collective-permute-start(f32[3,1,2,256]{3,2,1,0:T(2,128)S(1)} %get-tuple-element.266), channel_id=1, source_target_pairs={{8,0},{16,8},{24,16},{9,1},{17,9},{25,17},{10,2},{18,10},{26,18},{... | collective-permute-start | bytes 18440 | tf_op jit(solution)/shard_map/ppermute | solution.py:25
  19.0 18.2 %all-to-all-start.1 = ((s32[1,8,256]{2,0,1:T(1,128)}), s32[1,8,256]{2,0,1:T(1,128)S(1)}, u32[]{:S(2)}, u32[]{:S(2)}) async-start(s32[1,8,256]{2,0,1:T(1,128)} %bitcast.18), calls=%async_computation.1 | async-start | bytes 16384 | tf_op jit(solution)/shard_map/all_to_all | solution.py:202
  25.4 5.4 %collective-permute-start.2 = (f32[3,4,1,256]{3,2,1,0:T(1,128)S(1)}, f32[3,4,1,256]{3,2,1,0:T(1,128)S(1)}, u32[]{:S(2)}, u32[]{:S(2)}) collective-permute-start(f32[3,4,1,256]{3,2,1,0:T(1,128)S(1)} %get-tuple-element.226), channel_id=1, source_target_pairs={{0,1},{1,2},{2,3},{3,4},{4,5},{5,6},{6,7},{8,9},{9,10},{10,11},{11... | collective-permute-start | bytes 36872 | tf_op jit(solution)/shard_map/ppermute | solution.py:22
  27.8 4.2 collective-permute-start.3
  37.2 11.6 %all-to-all-start = ((f32[6,8,256]{2,0,1:T(8,128)}), f32[6,8,256]{2,0,1:T(8,128)S(1)}, u32[]{:S(2)}, u32[]{:S(2)}) async-start(f32[6,8,256]{2,0,1:T(8,128)} %copy.26), calls=%async_computation | async-start | bytes 131072 | tf_op jit(solution)/shard_map/all_to_all | solution.py:201
  96.6 29.3 %copy-start.4 = (f32[3,2,2,256]{3,2,1,0:T(2,128)S(1)}, f32[3,2,2,256]{3,2,1,0:T(2,128)}, u32[]{:S(2)}) copy-start(f32[3,2,2,256]{3,2,1,0:T(2,128)} %param.11) | copy-start | bytes 36868
  96.6 16.0 %all-to-all-start.2 = ((f32[42,8,256]{2,0,1:T(8,128)}), f32[42,8,256]{2,0,1:T(8,128)S(1)}, u32[]{:S(2)}, u32[]{:S(2)}) async-start(f32[42,8,256]{2,0,1:T(8,128)} %copy.27), calls=%async_computation.2 | async-start | bytes 786432 | tf_op jit(solution)/shard_map/all_to_all | solution.py:215
  116.1 6.6 %collective-permute-start.4 = (f32[42,1,2,256]{3,2,1,0:T(2,128)S(1)}, f32[42,1,2,256]{3,2,1,0:T(2,128)S(1)}, u32[]{:S(2)}, u32[]{:S(2)}) collective-permute-start(f32[42,1,2,256]{3,2,1,0:T(2,128)S(1)} %slice.1305), channel_id=1, source_target_pairs={{0,8},{8,16},{16,24},{1,9},{9,17},{17,25},{2,10},{10,18},{18,26},{... | collective-permute-start | bytes 258056 | tf_op jit(solution)/shard_map/ppermute | solution.py:33
  122.9 2.3 collective-permute-start.5
  126.1 5.6 %collective-permute-start.6 = (f32[3,1,2,256]{3,2,1,0:T(2,128)S(1)}, f32[3,1,2,256]{3,2,1,0:T(2,128)S(1)}, u32[]{:S(2)}, u32[]{:S(2)}) collective-permute-start(f32[3,1,2,256]{3,2,1,0:T(2,128)S(1)} %get-tuple-element.259), channel_id=1, source_target_pairs={{0,8},{8,16},{16,24},{1,9},{9,17},{17,25},{2,10},{10,18},{18,26},{... | collective-permute-start | bytes 18440 | tf_op jit(solution)/shard_map/ppermute | solution.py:22
  130.4 6.8 %collective-permute-start.7 = (f32[3,1,2,256]{3,2,1,0:T(2,128)S(1)}, f32[3,1,2,256]{3,2,1,0:T(2,128)S(1)}, u32[]{:S(2)}, u32[]{:S(2)}) collective-permute-start(f32[3,1,2,256]{3,2,1,0:T(2,128)S(1)} %get-tuple-element.260), channel_id=1, source_target_pairs={{8,0},{16,8},{24,16},{9,1},{17,9},{25,17},{10,2},{18,10},{26,18},{... | collective-permute-start | bytes 18440 | tf_op jit(solution)/shard_map/ppermute | solution.py:25
  137.2 3.5 collective-permute-start.8
  139.3 6.1 %collective-permute-start.9 = (f32[3,4,1,256]{3,2,1,0:T(1,128)S(1)}, f32[3,4,1,256]{3,2,1,0:T(1,128)S(1)}, u32[]{:S(2)}, u32[]{:S(2)}) collective-permute-start(f32[3,4,1,256]{3,2,1,0:T(1,128)S(1)} %get-tuple-element.224), channel_id=1, source_target_pairs={{1,0},{2,1},{3,2},{4,3},{5,4},{6,5},{7,6},{9,8},{10,9},{11,10},{12... | collective-permute-start | bytes 36872 | tf_op jit(solution)/shard_map/ppermute | solution.py:25
  191.6 5.5 %collective-permute-start.10 = (f32[3,1,2,256]{3,2,1,0:T(2,128)S(1)}, f32[3,1,2,256]{3,2,1,0:T(2,128)S(1)}, u32[]{:S(2)}, u32[]{:S(2)}) collective-permute-start(f32[3,1,2,256]{3,2,1,0:T(2,128)S(1)} %get-tuple-element.257), channel_id=1, source_target_pairs={{0,8},{8,16},{16,24},{1,9},{9,17},{17,25},{2,10},{10,18},{18,26},{... | collective-permute-start | bytes 18440 | tf_op jit(solution)/shard_map/ppermute | solution.py:22
  195.8 5.5 %collective-permute-start.11 = (f32[3,1,2,256]{3,2,1,0:T(2,128)S(1)}, f32[3,1,2,256]{3,2,1,0:T(2,128)S(1)}, u32[]{:S(2)}, u32[]{:S(2)}) collective-permute-start(f32[3,1,2,256]{3,2,1,0:T(2,128)S(1)} %get-tuple-element.258), channel_id=1, source_target_pairs={{8,0},{16,8},{24,16},{9,1},{17,9},{25,17},{10,2},{18,10},{26,18},{... | collective-permute-start | bytes 18440 | tf_op jit(solution)/shard_map/ppermute | solution.py:25
  201.4 2.6 collective-permute-start.12
  202.7 3.8 collective-permute-start.13
  255.5 5.5 %collective-permute-start.14 = (f32[3,1,2,256]{3,2,1,0:T(2,128)S(1)}, f32[3,1,2,256]{3,2,1,0:T(2,128)S(1)}, u32[]{:S(2)}, u32[]{:S(2)}) collective-permute-start(f32[3,1,2,256]{3,2,1,0:T(2,128)S(1)} %get-tuple-element.255), channel_id=1, source_target_pairs={{0,8},{8,16},{16,24},{1,9},{9,17},{17,25},{2,10},{10,18},{18,26},{... | collective-permute-start | bytes 18440 | tf_op jit(solution)/shard_map/ppermute | solution.py:22
  259.7 5.5 %collective-permute-start.15 = (f32[3,1,2,256]{3,2,1,0:T(2,128)S(1)}, f32[3,1,2,256]{3,2,1,0:T(2,128)S(1)}, u32[]{:S(2)}, u32[]{:S(2)}) collective-permute-start(f32[3,1,2,256]{3,2,1,0:T(2,128)S(1)} %get-tuple-element.256), channel_id=1, source_target_pairs={{8,0},{16,8},{24,16},{9,1},{17,9},{25,17},{10,2},{18,10},{26,18},{... | collective-permute-start | bytes 18440 | tf_op jit(solution)/shard_map/ppermute | solution.py:25
  265.2 2.6 collective-permute-start.16
  266.5 3.8 collective-permute-start.17
  318.8 5.5 %collective-permute-start.18 = (f32[3,1,2,256]{3,2,1,0:T(2,128)S(1)}, f32[3,1,2,256]{3,2,1,0:T(2,128)S(1)}, u32[]{:S(2)}, u32[]{:S(2)}) collective-permute-start(f32[3,1,2,256]{3,2,1,0:T(2,128)S(1)} %get-tuple-element.253), channel_id=1, source_target_pairs={{0,8},{8,16},{16,24},{1,9},{9,17},{17,25},{2,10},{10,18},{18,26},{... | collective-permute-start | bytes 18440 | tf_op jit(solution)/shard_map/ppermute | solution.py:22
  323.0 5.5 %collective-permute-start.19 = (f32[3,1,2,256]{3,2,1,0:T(2,128)S(1)}, f32[3,1,2,256]{3,2,1,0:T(2,128)S(1)}, u32[]{:S(2)}, u32[]{:S(2)}) collective-permute-start(f32[3,1,2,256]{3,2,1,0:T(2,128)S(1)} %get-tuple-element.254), channel_id=1, source_target_pairs={{8,0},{16,8},{24,16},{9,1},{17,9},{25,17},{10,2},{18,10},{26,18},{... | collective-permute-start | bytes 18440 | tf_op jit(solution)/shard_map/ppermute | solution.py:25
  328.5 2.6 collective-permute-start.20
  329.8 3.8 collective-permute-start.21
  382.2 5.5 %collective-permute-start.22 = (f32[3,1,2,256]{3,2,1,0:T(2,128)S(1)}, f32[3,1,2,256]{3,2,1,0:T(2,128)S(1)}, u32[]{:S(2)}, u32[]{:S(2)}) collective-permute-start(f32[3,1,2,256]{3,2,1,0:T(2,128)S(1)} %get-tuple-element.251), channel_id=1, source_target_pairs={{0,8},{8,16},{16,24},{1,9},{9,17},{17,25},{2,10},{10,18},{18,26},{... | collective-permute-start | bytes 18440 | tf_op jit(solution)/shard_map/ppermute | solution.py:22
  386.4 5.5 %collective-permute-start.23 = (f32[3,1,2,256]{3,2,1,0:T(2,128)S(1)}, f32[3,1,2,256]{3,2,1,0:T(2,128)S(1)}, u32[]{:S(2)}, u32[]{:S(2)}) collective-permute-start(f32[3,1,2,256]{3,2,1,0:T(2,128)S(1)} %get-tuple-element.252), channel_id=1, source_target_pairs={{8,0},{16,8},{24,16},{9,1},{17,9},{25,17},{10,2},{18,10},{26,18},{... | collective-permute-start | bytes 18440 | tf_op jit(solution)/shard_map/ppermute | solution.py:25
  392.0 2.6 collective-permute-start.24
  393.3 3.8 collective-permute-start.25
  (4 other events, 43.2 us)
where the time goes:
time: 449 us; the launch traced here: 446 us
  blocking collectives  212 us (47%)
  starting transfers between devices  71.2 us (16%)
  waiting for transfers between devices  59.1 us (13%)
  matrix products  46 us (10%)
  between operations  20.8 us (5%)
  other arithmetic  19.8 us (4%)
  local copies, waits for them, and re-layouts  17 us (4%)
    psum x5, blocking collectives, two_products(): lax.psum((jnp.sum(residual * residual), jnp.sum(residual * image)), ('mac...  212 us
    ppermute x12, waiting for transfers between devices, with_halo(): lax.ppermute(lax.slice_in_dim(block, 0, width, axis=dim), axis, backward)  38.2 us
    dot_general x4, matrix products, micro_solve(): jnp.dot(misfit.astype(jnp.bfloat16), precond, preferred_element_type=jnp....  36.1 us
    ppermute x12, starting transfers between devices, with_halo(): lax.ppermute(lax.slice_in_dim(block, block.shape[dim] - width, None, axis...  35.5 us
    ppermute x12, starting transfers between devices, with_halo(): lax.ppermute(lax.slice_in_dim(block, 0, width, axis=dim), axis, backward)  15.5 us
    all_to_all x1, waiting for transfers between devices, shards(): lax.all_to_all(rows, 'micro', split_axis=1, concat_axis=1, tiled=True)  12.3 us
  transfers between devices with their start and end apart: 29, of which 15 were waited for; matrix products, arithmetic and copies ran while one was open for 4% of the time, Pallas kernels for 0%

commit v1 on v0

--- a/solution.py
+++ b/solution.py
@@ -165,7 +165,12 @@
 
 
 def two_products(residual, image):
-    return lax.psum((jnp.sum(residual * residual), jnp.sum(residual * image)), ("macro", "micro"))
+
+    def _prepare_numbers(vals):
+        piece_now = lax.psum(vals, "micro")
+        return lax.psum(piece_now, "macro")
+
+    return _prepare_numbers((jnp.sum(residual * residual), jnp.sum(residual * image)))
 
 
 def shards(

time: 449 us -> 360 us (0.80)
  blocking collectives: 212 us -> 132 us
  starting transfers between devices: 71.2 us -> 61.1 us
    psum x5 -> x10, blocking collectives: 212 us -> 132 us  [the longest x5 77.4 us: _prepare_numbers(): piece_now = lax.psum(vals, 'micro')]
    ppermute x12, starting transfers between devices: 35.5 us -> 25.4 us  [with_halo(): lax.ppermute(lax.slice_in_dim(block, block.shape[dim] - width, None, axis...]
  transfers between devices with their start and end apart: 29 -> 29, of which waited for: 15 -> 15; matrix products, arithmetic and copies ran while one was open for 4% -> 5% of each run, Pallas kernels for 0% -> 0%
where the time goes in v1:
time: 360 us; the launch traced here: 358 us
  blocking collectives  132 us (37%)
  starting transfers between devices  61.1 us (17%)
  waiting for transfers between devices  60.8 us (17%)
  matrix products  45.9 us (13%)
  between operations  21.1 us (6%)
  other arithmetic  19.8 us (6%)
  local copies, waits for them, and re-layouts  17 us (5%)
    psum x5, blocking collectives, _prepare_numbers(): piece_now = lax.psum(vals, 'micro')  77.4 us
    psum x5, blocking collectives, _prepare_numbers(): return lax.psum(piece_now, 'macro')  55.1 us
    ppermute x12, waiting for transfers between devices, with_halo(): lax.ppermute(lax.slice_in_dim(block, 0, width, axis=dim), axis, backward)  39.8 us
    dot_general x4, matrix products, micro_solve(): jnp.dot(misfit.astype(jnp.bfloat16), precond, preferred_element_type=jnp....  36 us
    ppermute x12, starting transfers between devices, with_halo(): lax.ppermute(lax.slice_in_dim(block, block.shape[dim] - width, None, axis...  25.4 us
    ppermute x12, starting transfers between devices, with_halo(): lax.ppermute(lax.slice_in_dim(block, 0, width, axis=dim), axis, backward)  15.5 us
    all_to_all x1, waiting for transfers between devices, shards(): lax.all_to_all(rows, 'micro', split_axis=1, concat_axis=1, tiled=True)  12.3 us
  transfers between devices with their start and end apart: 29, of which 15 were waited for; matrix products, arithmetic and copies ran while one was open for 5% of the time, Pallas kernels for 0%

profile of v1, /device:TPU:0, one launch (start us, length us, event | category | flops | bytes accessed | tf_op | source)
XLA Modules:
  0.0 358.2 jit_solution(8629706075465855807)
XLA Ops:
  1.4 4.9 %collective-permute-start = (f32[3,1,2,256]{3,2,1,0:T(2,128)S(1)}, f32[3,1,2,256]{3,2,1,0:T(2,128)S(1)}, u32[]{:S(2)}, u32[]{:S(2)}) collective-permute-start(f32[3,1,2,256]{3,2,1,0:T(2,128)S(1)} %get-tuple-element.277), channel_id=1, source_target_pairs={{0,8},{8,16},{16,24},{1,9},{9,17},{17,25},{2,10},{10,18},{18,26},{... | collective-permute-start | bytes 18440 | tf_op jit(solution)/shard_map/ppermute | solution.py:22
  14.0 5.0 %scatter_custom_fusion.1 = s32[2048]{0:T(1024)} fusion(s32[1024]{0:T(1024)S(1)} %broadcast_select_fusion.1, s32[1024]{0:T(1024)} %bitcast.117, s32[]{:T(128)} %constant.19.clone.1), kind=kCustom, calls=%fused_computation.834 | custom fusion | bytes 8704
  19.0 4.9 %all-to-all-start.1 = ((s32[1,8,256]{2,0,1:T(1,128)}), s32[1,8,256]{2,0,1:T(1,128)S(1)}, u32[]{:S(2)}, u32[]{:S(2)}) async-start(s32[1,8,256]{2,0,1:T(1,128)} %bitcast.18), calls=%async_computation.1 | async-start | bytes 16384 | tf_op jit(solution)/shard_map/all_to_all | solution.py:207
  32.9 3.3 scatter_custom_fusion
  37.2 5.7 %all-to-all-start = ((f32[6,8,256]{2,0,1:T(8,128)}), f32[6,8,256]{2,0,1:T(8,128)S(1)}, u32[]{:S(2)}, u32[]{:S(2)}) async-start(f32[6,8,256]{2,0,1:T(8,128)} %copy.26), calls=%async_computation | async-start | bytes 131072 | tf_op jit(solution)/shard_map/all_to_all | solution.py:206
  43.1 5.8 %all-to-all-done = f32[6,8,256]{2,0,1:T(8,128)S(1)} async-done(((f32[6,8,256]{2,0,1:T(8,128)}), f32[6,8,256]{2,0,1:T(8,128)S(1)}, u32[]{:S(2)}, u32[]{:S(2)}) %all-to-all-start) | async-done | bytes 49184 | tf_op jit(solution)/shard_map/all_to_all | solution.py:206
  51.5 6.6 %subtract_select_fusion.3 = f32[2048,512]{1,0:T(8,128)} fusion(pred[2048]{0:T(1024)(128)(4,1)S(1)} %gt.63, f32[2048,512]{1,0:T(8,128)} %fusion.206, bf16[1,512,512]{2,1,0:T(8,128)(2,1)S(1)} %copy-done, bf16[1,512,512]{2,1,0:T(8,128)(2,1)S(1)} %copy-done.6), kind=kOutput, calls=%fused_computation.13 | convolution fusion | flops 2152726528 | bytes 9439232 | tf_op jit(solution)/shard_map/dot_general | solution.py:112
  58.1 9.7 %subtract_select_fusion.2 = f32[2048,512]{1,0:T(8,128)} fusion(f32[2048,512]{1,0:T(8,128)} %subtract_select_fusion.3, pred[2048]{0:T(1024)(128)(4,1)S(1)} %gt.60, f32[2048,512]{1,0:T(8,128)} %fusion.206, bf16[1,512,512]{2,1,0:T(8,128)(2,1)S(1)} %copy-done, bf16[1,512,512]{2,1,0:T(8,128)(2,1)S(1)} %copy-done.6), kind=kOutput, calls=%fused_computation.5 | convolution fusion | flops 2155872256 | bytes 13633536 | tf_op jit(solution)/shard_map/dot_general | solution.py:112
  67.8 10.0 %subtract_select_fusion.1 = f32[2048,512]{1,0:T(8,128)} fusion(f32[2048,512]{1,0:T(8,128)} %subtract_select_fusion.2, pred[2048]{0:T(1024)(128)(4,1)S(1)} %gt.57, f32[2048,512]{1,0:T(8,128)} %fusion.206, bf16[1,512,512]{2,1,0:T(8,128)(2,1)S(1)} %copy-done, bf16[1,512,512]{2,1,0:T(8,128)(2,1)S(1)} %copy-done.6), kind=kOutput, calls=%fused_computation.4 | convolution fusion | flops 2155872256 | bytes 13633536 | tf_op jit(solution)/shard_map/dot_general | solution.py:112
  77.8 9.7 %subtract_select_fusion = f32[2048,512]{1,0:T(8,128)} fusion(f32[2048,512]{1,0:T(8,128)} %subtract_select_fusion.1, pred[2048]{0:T(1024)(128)(4,1)S(1)} %gt.54, f32[2048,512]{1,0:T(8,128)} %fusion.206, bf16[1,512,512]{2,1,0:T(8,128)(2,1)S(1)} %copy-done, bf16[1,512,512]{2,1,0:T(8,128)(2,1)S(1)} %copy-done.6), kind=kOutput, calls=%fused_computation.3 | convolution fusion | flops 2155872256 | bytes 13633536 | tf_op jit(solution)/shard_map/dot_general | solution.py:112
  87.7 3.0 fusion.7
  91.1 4.2 %fusion.4 = f32[36,2048]{1,0:T(8,128)S(1)} fusion(f32[512,36]{0,1:T(8,128)S(1)} %stack.124, f32[2048,512]{1,0:T(8,128)S(1)} %copy-done.1, f32[36]{0:T(128)S(1)} %stack.129), kind=kOutput, calls=%fused_computation.15 | convolution fusion | flops 455155712 | bytes 4563088 | tf_op jit(solution)/shard_map/dot_general | solution.py:136
  96.4 3.6 %all-to-all-start.2 = ((f32[42,8,256]{2,0,1:T(8,128)}), f32[42,8,256]{2,0,1:T(8,128)S(1)}, u32[]{:S(2)}, u32[]{:S(2)}) async-start(f32[42,8,256]{2,0,1:T(8,128)} %copy.27), calls=%async_computation.2 | async-start | bytes 786432 | tf_op jit(solution)/shard_map/all_to_all | solution.py:220
  100.2 12.3 %all-to-all-done.2 = f32[42,8,256]{2,0,1:T(8,128)S(1)} async-done(((f32[42,8,256]{2,0,1:T(8,128)}), f32[42,8,256]{2,0,1:T(8,128)S(1)}, u32[]{:S(2)}, u32[]{:S(2)}) %all-to-all-start.2) | async-done | bytes 344096 | tf_op jit(solution)/shard_map/all_to_all | solution.py:220
  116.0 4.5 %collective-permute-start.4 = (f32[42,1,2,256]{3,2,1,0:T(2,128)S(1)}, f32[42,1,2,256]{3,2,1,0:T(2,128)S(1)}, u32[]{:S(2)}, u32[]{:S(2)}) collective-permute-start(f32[42,1,2,256]{3,2,1,0:T(2,128)S(1)} %slice.1305), channel_id=1, source_target_pairs={{0,8},{8,16},{16,24},{1,9},{9,17},{17,25},{2,10},{10,18},{18,26},{... | collective-permute-start | bytes 258056 | tf_op jit(solution)/shard_map/ppermute | solution.py:33
  126.0 4.3 %collective-permute-start.6 = (f32[3,1,2,256]{3,2,1,0:T(2,128)S(1)}, f32[3,1,2,256]{3,2,1,0:T(2,128)S(1)}, u32[]{:S(2)}, u32[]{:S(2)}) collective-permute-start(f32[3,1,2,256]{3,2,1,0:T(2,128)S(1)} %get-tuple-element.269), channel_id=1, source_target_pairs={{0,8},{8,16},{16,24},{1,9},{9,17},{17,25},{2,10},{10,18},{18,26},{... | collective-permute-start | bytes 18440 | tf_op jit(solution)/shard_map/ppermute | solution.py:22
  131.6 5.5 %collective-permute-done.7 = f32[3,1,2,256]{3,2,1,0:T(2,128)S(1)} collective-permute-done((f32[3,1,2,256]{3,2,1,0:T(2,128)S(1)}, f32[3,1,2,256]{3,2,1,0:T(2,128)S(1)}, u32[]{:S(2)}, u32[]{:S(2)}) %collective-permute-start.7) | collective-permute-done | bytes 6176 | tf_op jit(solution)/shard_map/ppermute | solution.py:25
  140.7 4.6 %collective-permute-done.9 = f32[3,4,1,256]{3,2,1,0:T(1,128)S(1)} collective-permute-done((f32[3,4,1,256]{3,2,1,0:T(1,128)S(1)}, f32[3,4,1,256]{3,2,1,0:T(1,128)S(1)}, u32[]{:S(2)}, u32[]{:S(2)}) %collective-permute-start.9) | collective-permute-done | bytes 12320 | tf_op jit(solution)/shard_map/ppermute | solution.py:25
  147.4 16.6 %all-reduce.59 = (f32[]{:T(128)}, f32[]{:T(128)}) all-reduce(f32[]{:T(128)} %get-tuple-element.11, f32[]{:T(128)} %get-tuple-element.10), channel_id=1, replica_groups=mesh['macro'=4,'micro'=8] {'micro'}, use_global_device_ids=true, to_apply=%region_6.7 | all-reduce | flops 2 | bytes 16 | tf_op jit(solution)/shard_map/psum | solution.py:170
  164.1 11.0 %all-reduce.64 = (f32[]{:T(128)}, f32[]{:T(128)}) all-reduce(f32[]{:T(128)} %get-tuple-element.24, f32[]{:T(128)} %get-tuple-element.25), channel_id=1, replica_groups=mesh['macro'=4,'micro'=8] {'macro'}, use_global_device_ids=true, to_apply=%region_7.8 | all-reduce | flops 2 | bytes 16 | tf_op jit(solution)/shard_map/psum | solution.py:171
  179.4 5.4 %collective-permute-done.11 = f32[3,1,2,256]{3,2,1,0:T(2,128)S(1)} collective-permute-done((f32[3,1,2,256]{3,2,1,0:T(2,128)S(1)}, f32[3,1,2,256]{3,2,1,0:T(2,128)S(1)}, u32[]{:S(2)}, u32[]{:S(2)}) %collective-permute-start.11) | collective-permute-done | bytes 6176 | tf_op jit(solution)/shard_map/ppermute | solution.py:25
  191.4 15.2 %all-reduce.58 = (f32[]{:T(128)}, f32[]{:T(128)}) all-reduce(f32[]{:T(128)} %get-tuple-element.9, f32[]{:T(128)} %get-tuple-element.8), channel_id=1, replica_groups=mesh['macro'=4,'micro'=8] {'micro'}, use_global_device_ids=true, to_apply=%region_13.14 | all-reduce | flops 2 | bytes 16 | tf_op jit(solution)/shard_map/psum | solution.py:170
  206.6 11.1 %all-reduce.63 = (f32[]{:T(128)}, f32[]{:T(128)}) all-reduce(f32[]{:T(128)} %get-tuple-element.22, f32[]{:T(128)} %get-tuple-element.23), channel_id=1, replica_groups=mesh['macro'=4,'micro'=8] {'macro'}, use_global_device_ids=true, to_apply=%region_14.15 | all-reduce | flops 2 | bytes 16 | tf_op jit(solution)/shard_map/psum | solution.py:171
  225.0 5.4 %collective-permute-done.15 = f32[3,1,2,256]{3,2,1,0:T(2,128)S(1)} collective-permute-done((f32[3,1,2,256]{3,2,1,0:T(2,128)S(1)}, f32[3,1,2,256]{3,2,1,0:T(2,128)S(1)}, u32[]{:S(2)}, u32[]{:S(2)}) %collective-permute-start.15) | collective-permute-done | bytes 6176 | tf_op jit(solution)/shard_map/ppermute | solution.py:25
  237.0 15.2 %all-reduce.57 = (f32[]{:T(128)}, f32[]{:T(128)}) all-reduce(f32[]{:T(128)} %get-tuple-element.7, f32[]{:T(128)} %get-tuple-element.6), channel_id=1, replica_groups=mesh['macro'=4,'micro'=8] {'micro'}, use_global_device_ids=true, to_apply=%region_20.21 | all-reduce | flops 2 | bytes 16 | tf_op jit(solution)/shard_map/psum | solution.py:170
  252.2 11.0 %all-reduce.62 = (f32[]{:T(128)}, f32[]{:T(128)}) all-reduce(f32[]{:T(128)} %get-tuple-element.20, f32[]{:T(128)} %get-tuple-element.21), channel_id=1, replica_groups=mesh['macro'=4,'micro'=8] {'macro'}, use_global_device_ids=true, to_apply=%region_21.22 | all-reduce | flops 2 | bytes 16 | tf_op jit(solution)/shard_map/psum | solution.py:171
  270.0 5.4 %collective-permute-done.19 = f32[3,1,2,256]{3,2,1,0:T(2,128)S(1)} collective-permute-done((f32[3,1,2,256]{3,2,1,0:T(2,128)S(1)}, f32[3,1,2,256]{3,2,1,0:T(2,128)S(1)}, u32[]{:S(2)}, u32[]{:S(2)}) %collective-permute-start.19) | collective-permute-done | bytes 6176 | tf_op jit(solution)/shard_map/ppermute | solution.py:25
  282.0 15.2 %all-reduce.56 = (f32[]{:T(128)}, f32[]{:T(128)}) all-reduce(f32[]{:T(128)} %get-tuple-element.5, f32[]{:T(128)} %get-tuple-element.4), channel_id=1, replica_groups=mesh['macro'=4,'micro'=8] {'micro'}, use_global_device_ids=true, to_apply=%region_27.28 | all-reduce | flops 2 | bytes 16 | tf_op jit(solution)/shard_map/psum | solution.py:170
  297.2 11.1 %all-reduce.61 = (f32[]{:T(128)}, f32[]{:T(128)}) all-reduce(f32[]{:T(128)} %get-tuple-element.18, f32[]{:T(128)} %get-tuple-element.19), channel_id=1, replica_groups=mesh['macro'=4,'micro'=8] {'macro'}, use_global_device_ids=true, to_apply=%region_28.29 | all-reduce | flops 2 | bytes 16 | tf_op jit(solution)/shard_map/psum | solution.py:171
  315.4 5.4 %collective-permute-done.23 = f32[3,1,2,256]{3,2,1,0:T(2,128)S(1)} collective-permute-done((f32[3,1,2,256]{3,2,1,0:T(2,128)S(1)}, f32[3,1,2,256]{3,2,1,0:T(2,128)S(1)}, u32[]{:S(2)}, u32[]{:S(2)}) %collective-permute-start.23) | collective-permute-done | bytes 6176 | tf_op jit(solution)/shard_map/ppermute | solution.py:25
  327.3 15.2 %all-reduce.55 = (f32[]{:T(128)}, f32[]{:T(128)}) all-reduce(f32[]{:T(128)} %get-tuple-element.3, f32[]{:T(128)} %get-tuple-element.2), channel_id=1, replica_groups=mesh['macro'=4,'micro'=8] {'micro'}, use_global_device_ids=true, to_apply=%region_34.35 | all-reduce | flops 2 | bytes 16 | tf_op jit(solution)/shard_map/psum | solution.py:170
  342.5 11.0 %all-reduce.60 = (f32[]{:T(128)}, f32[]{:T(128)}) all-reduce(f32[]{:T(128)} %get-tuple-element.16, f32[]{:T(128)} %get-tuple-element.17), channel_id=1, replica_groups=mesh['macro'=4,'micro'=8] {'macro'}, use_global_device_ids=true, to_apply=%region_35.36 | all-reduce | flops 2 | bytes 16 | tf_op jit(solution)/shard_map/psum | solution.py:171
  (293 shorter events, 75.5 us)
Async XLA Ops:
  0.6 50.9 %copy-start = (bf16[1,512,512]{2,1,0:T(8,128)(2,1)S(1)}, bf16[1,512,512]{2,1,0:T(8,128)(2,1)}, u32[]{:S(2)}) copy-start(bf16[1,512,512]{2,1,0:T(8,128)(2,1)} %param.15) | copy-start | bytes 1572868
  0.6 48.2 %copy-start.5 = (bf16[1,6,512]{2,1,0:T(8,128)(2,1)S(1)}, bf16[1,6,512]{2,1,0:T(8,128)(2,1)}, u32[]{:S(2)}) copy-start(bf16[1,6,512]{2,1,0:T(8,128)(2,1)} %param.16) | copy-start | bytes 18436
  1.4 23.2 %collective-permute-start = (f32[3,1,2,256]{3,2,1,0:T(2,128)S(1)}, f32[3,1,2,256]{3,2,1,0:T(2,128)S(1)}, u32[]{:S(2)}, u32[]{:S(2)}) collective-permute-start(f32[3,1,2,256]{3,2,1,0:T(2,128)S(1)} %get-tuple-element.277), channel_id=1, source_target_pairs={{0,8},{8,16},{16,24},{1,9},{9,17},{17,25},{2,10},{10,18},{18,26},{... | collective-permute-start | bytes 18440 | tf_op jit(solution)/shard_map/ppermute | solution.py:22
  6.3 19.1 %collective-permute-start.1 = (f32[3,1,2,256]{3,2,1,0:T(2,128)S(1)}, f32[3,1,2,256]{3,2,1,0:T(2,128)S(1)}, u32[]{:S(2)}, u32[]{:S(2)}) collective-permute-start(f32[3,1,2,256]{3,2,1,0:T(2,128)S(1)} %get-tuple-element.276), channel_id=1, source_target_pairs={{8,0},{16,8},{24,16},{9,1},{17,9},{25,17},{10,2},{18,10},{26,18},{... | collective-permute-start | bytes 18440 | tf_op jit(solution)/shard_map/ppermute | solution.py:25
  19.0 18.2 %all-to-all-start.1 = ((s32[1,8,256]{2,0,1:T(1,128)}), s32[1,8,256]{2,0,1:T(1,128)S(1)}, u32[]{:S(2)}, u32[]{:S(2)}) async-start(s32[1,8,256]{2,0,1:T(1,128)} %bitcast.18), calls=%async_computation.1 | async-start | bytes 16384 | tf_op jit(solution)/shard_map/all_to_all | solution.py:207
  25.4 5.4 %collective-permute-start.2 = (f32[3,4,1,256]{3,2,1,0:T(1,128)S(1)}, f32[3,4,1,256]{3,2,1,0:T(1,128)S(1)}, u32[]{:S(2)}, u32[]{:S(2)}) collective-permute-start(f32[3,4,1,256]{3,2,1,0:T(1,128)S(1)} %get-tuple-element.236), channel_id=1, source_target_pairs={{0,1},{1,2},{2,3},{3,4},{4,5},{5,6},{6,7},{8,9},{9,10},{10,11},{11... | collective-permute-start | bytes 36872 | tf_op jit(solution)/shard_map/ppermute | solution.py:22
  27.8 4.2 %collective-permute-start.3 = (f32[3,4,1,256]{3,2,1,0:T(1,128)S(1)}, f32[3,4,1,256]{3,2,1,0:T(1,128)S(1)}, u32[]{:S(2)}, u32[]{:S(2)}) collective-permute-start(f32[3,4,1,256]{3,2,1,0:T(1,128)S(1)} %get-tuple-element.237), channel_id=1, source_target_pairs={{1,0},{2,1},{3,2},{4,3},{5,4},{6,5},{7,6},{9,8},{10,9},{11,10},{12... | collective-permute-start | bytes 36872 | tf_op jit(solution)/shard_map/ppermute | solution.py:25
  37.2 11.6 %all-to-all-start = ((f32[6,8,256]{2,0,1:T(8,128)}), f32[6,8,256]{2,0,1:T(8,128)S(1)}, u32[]{:S(2)}, u32[]{:S(2)}) async-start(f32[6,8,256]{2,0,1:T(8,128)} %copy.26), calls=%async_computation | async-start | bytes 131072 | tf_op jit(solution)/shard_map/all_to_all | solution.py:206
  96.4 29.3 %copy-start.4 = (f32[3,2,2,256]{3,2,1,0:T(2,128)S(1)}, f32[3,2,2,256]{3,2,1,0:T(2,128)}, u32[]{:S(2)}) copy-start(f32[3,2,2,256]{3,2,1,0:T(2,128)} %param.11) | copy-start | bytes 36868
  96.4 16.0 %all-to-all-start.2 = ((f32[42,8,256]{2,0,1:T(8,128)}), f32[42,8,256]{2,0,1:T(8,128)S(1)}, u32[]{:S(2)}, u32[]{:S(2)}) async-start(f32[42,8,256]{2,0,1:T(8,128)} %copy.27), calls=%async_computation.2 | async-start | bytes 786432 | tf_op jit(solution)/shard_map/all_to_all | solution.py:220
  116.0 6.6 %collective-permute-start.4 = (f32[42,1,2,256]{3,2,1,0:T(2,128)S(1)}, f32[42,1,2,256]{3,2,1,0:T(2,128)S(1)}, u32[]{:S(2)}, u32[]{:S(2)}) collective-permute-start(f32[42,1,2,256]{3,2,1,0:T(2,128)S(1)} %slice.1305), channel_id=1, source_target_pairs={{0,8},{8,16},{16,24},{1,9},{9,17},{17,25},{2,10},{10,18},{18,26},{... | collective-permute-start | bytes 258056 | tf_op jit(solution)/shard_map/ppermute | solution.py:33
  122.8 2.3 collective-permute-start.5
  126.0 5.6 %collective-permute-start.6 = (f32[3,1,2,256]{3,2,1,0:T(2,128)S(1)}, f32[3,1,2,256]{3,2,1,0:T(2,128)S(1)}, u32[]{:S(2)}, u32[]{:S(2)}) collective-permute-start(f32[3,1,2,256]{3,2,1,0:T(2,128)S(1)} %get-tuple-element.269), channel_id=1, source_target_pairs={{0,8},{8,16},{16,24},{1,9},{9,17},{17,25},{2,10},{10,18},{18,26},{... | collective-permute-start | bytes 18440 | tf_op jit(solution)/shard_map/ppermute | solution.py:22
  130.3 6.8 %collective-permute-start.7 = (f32[3,1,2,256]{3,2,1,0:T(2,128)S(1)}, f32[3,1,2,256]{3,2,1,0:T(2,128)S(1)}, u32[]{:S(2)}, u32[]{:S(2)}) collective-permute-start(f32[3,1,2,256]{3,2,1,0:T(2,128)S(1)} %get-tuple-element.270), channel_id=1, source_target_pairs={{8,0},{16,8},{24,16},{9,1},{17,9},{25,17},{10,2},{18,10},{26,18},{... | collective-permute-start | bytes 18440 | tf_op jit(solution)/shard_map/ppermute | solution.py:25
  137.1 3.5 collective-permute-start.8
  139.2 6.1 %collective-permute-start.9 = (f32[3,4,1,256]{3,2,1,0:T(1,128)S(1)}, f32[3,4,1,256]{3,2,1,0:T(1,128)S(1)}, u32[]{:S(2)}, u32[]{:S(2)}) collective-permute-start(f32[3,4,1,256]{3,2,1,0:T(1,128)S(1)} %get-tuple-element.234), channel_id=1, source_target_pairs={{1,0},{2,1},{3,2},{4,3},{5,4},{6,5},{7,6},{9,8},{10,9},{11,10},{12... | collective-permute-start | bytes 36872 | tf_op jit(solution)/shard_map/ppermute | solution.py:25
  176.4 3.0 collective-permute-start.10
  178.1 6.7 %collective-permute-start.11 = (f32[3,1,2,256]{3,2,1,0:T(2,128)S(1)}, f32[3,1,2,256]{3,2,1,0:T(2,128)S(1)}, u32[]{:S(2)}, u32[]{:S(2)}) collective-permute-start(f32[3,1,2,256]{3,2,1,0:T(2,128)S(1)} %get-tuple-element.268), channel_id=1, source_target_pairs={{8,0},{16,8},{24,16},{9,1},{17,9},{25,17},{10,2},{18,10},{26,18},{... | collective-permute-start | bytes 18440 | tf_op jit(solution)/shard_map/ppermute | solution.py:25
  184.8 2.6 collective-permute-start.12
  186.1 3.1 collective-permute-start.13
  222.1 3.0 collective-permute-start.14
  223.7 6.7 %collective-permute-start.15 = (f32[3,1,2,256]{3,2,1,0:T(2,128)S(1)}, f32[3,1,2,256]{3,2,1,0:T(2,128)S(1)}, u32[]{:S(2)}, u32[]{:S(2)}) collective-permute-start(f32[3,1,2,256]{3,2,1,0:T(2,128)S(1)} %get-tuple-element.266), channel_id=1, source_target_pairs={{8,0},{16,8},{24,16},{9,1},{17,9},{25,17},{10,2},{18,10},{26,18},{... | collective-permute-start | bytes 18440 | tf_op jit(solution)/shard_map/ppermute | solution.py:25
  230.4 2.6 collective-permute-start.16
  231.7 3.1 collective-permute-start.17
  267.0 3.0 collective-permute-start.18
  268.6 6.7 %collective-permute-start.19 = (f32[3,1,2,256]{3,2,1,0:T(2,128)S(1)}, f32[3,1,2,256]{3,2,1,0:T(2,128)S(1)}, u32[]{:S(2)}, u32[]{:S(2)}) collective-permute-start(f32[3,1,2,256]{3,2,1,0:T(2,128)S(1)} %get-tuple-element.264), channel_id=1, source_target_pairs={{8,0},{16,8},{24,16},{9,1},{17,9},{25,17},{10,2},{18,10},{26,18},{... | collective-permute-start | bytes 18440 | tf_op jit(solution)/shard_map/ppermute | solution.py:25
  275.4 2.6 collective-permute-start.20
  276.7 3.1 collective-permute-start.21
  312.4 3.0 collective-permute-start.22
  314.0 6.7 %collective-permute-start.23 = (f32[3,1,2,256]{3,2,1,0:T(2,128)S(1)}, f32[3,1,2,256]{3,2,1,0:T(2,128)S(1)}, u32[]{:S(2)}, u32[]{:S(2)}) collective-permute-start(f32[3,1,2,256]{3,2,1,0:T(2,128)S(1)} %get-tuple-element.262), channel_id=1, source_target_pairs={{8,0},{16,8},{24,16},{9,1},{17,9},{25,17},{10,2},{18,10},{26,18},{... | collective-permute-start | bytes 18440 | tf_op jit(solution)/shard_map/ppermute | solution.py:25
  320.8 2.6 collective-permute-start.24
  322.1 3.1 collective-permute-start.25
  (4 other events, 43.2 us)
